TPU v7x, 32 devices: a whole 2x2x4 slice. The times are simulated.
32 devices in a mesh: row: 8 (over z, x), col: 4 (over y, core).
Axes of the slice: x: 2, y: 2, z: 4, core: 2. Of those that a mesh axis runs over, the one named last changes fastest.
Arguments:
- matrix: float32 [16384, 16384], P('row', 'col'), may hold values from -300 to 300, as said below
Outputs:
- trailing: float32 [16384, 16384], P('row', 'col')
- reflectors: float32 [16384, 8], P('row')
Inputs may be any that keep to these rules, and one draw needn't show every extreme that they name: matrix is exactly symmetric.
All inputs are finite; a program needn't handle non-finite values.
Results may differ from a plain program's by a relative error of at most 0.00021.
Values sent between devices are 32-bit elements; how exact they have to be, the bound alone decides.
A program may use at most 128 MiB of HBM per device.

v0:
```python
import jax
import jax.numpy as jnp
from jax import lax
from jax.sharding import PartitionSpec as P

N = 16384
COLS = 8


def from_root(block, axis, source):
    block = jnp.where(lax.axis_index(axis) == source, block, jnp.zeros_like(block))
    return lax.psum(block, axis)


def precise_dot(operand, factor):
    return jnp.dot(
        operand, factor, precision=lax.Precision.HIGHEST, preferred_element_type=jnp.float32
    )


def local(matrix):
    rows_local = matrix.shape[0]
    cols_local = matrix.shape[1]
    row_index = lax.axis_index("row")
    col_index = lax.axis_index("col")
    panel = from_root(matrix[:, :COLS], "col", 0)
    whole_panel = lax.all_gather(panel, "row", axis=0, tiled=True)
    all_ids = jnp.arange(whole_panel.shape[0], dtype=jnp.int32)
    reflect = jnp.zeros((N, COLS), jnp.float32)
    companion = jnp.zeros((N, COLS), jnp.float32)
    for column in range(COLS):
        reflect_rows = lax.dynamic_slice_in_dim(reflect, row_index * rows_local, rows_local, 0)
        companion_rows = lax.dynamic_slice_in_dim(companion, row_index * rows_local, rows_local, 0)
        current = (
            whole_panel[:, column]
            - precise_dot(reflect, companion[column])
            - precise_dot(companion, reflect[column])
        )
        below_whole = jnp.where(all_ids > column, current, 0.0)
        squared = jnp.sum(below_whole * below_whole)
        leading = jnp.sum(jnp.where(all_ids == column + 1, current, 0.0))
        length = jnp.sqrt(squared)
        vector = below_whole + jnp.where(all_ids == column + 1, length, 0.0)
        scaling = 1.0 / (length * (length + leading))
        vector_rows = lax.dynamic_slice_in_dim(vector, row_index * rows_local, rows_local, 0)
        vector_cols = lax.dynamic_slice_in_dim(vector, col_index * cols_local, cols_local, 0)
        weight_comp = precise_dot(companion.T, vector)
        weight_refl = precise_dot(reflect.T, vector)
        row_image = lax.psum(precise_dot(matrix, vector_cols), "col")
        pushed = scaling * (
            row_image
            - precise_dot(reflect_rows, weight_comp)
            - precise_dot(companion_rows, weight_refl)
        )
        inner_product = lax.psum(jnp.sum(pushed * vector_rows), "row")
        update_rows = pushed - 0.5 * scaling * inner_product * vector_rows
        update = lax.all_gather(update_rows, "row", axis=0, tiled=True)
        reflect = reflect.at[:, column].set(vector)
        companion = companion.at[:, column].set(update)
    reflect_rows = lax.dynamic_slice_in_dim(reflect, row_index * rows_local, rows_local, 0)
    companion_rows = lax.dynamic_slice_in_dim(companion, row_index * rows_local, rows_local, 0)
    reflect_cols = lax.dynamic_slice_in_dim(reflect, col_index * cols_local, cols_local, 0)
    companion_cols = lax.dynamic_slice_in_dim(companion, col_index * cols_local, cols_local, 0)
    trailing = (
        matrix
        - precise_dot(reflect_rows, companion_cols.T)
        - precise_dot(companion_rows, reflect_cols.T)
    )
    return (trailing, reflect_rows)


def solution(mesh):
    placed = (P("row", "col"),)
    return jax.shard_map(
        local,
        mesh=mesh,
        in_specs=placed,
        out_specs=(P("row", "col"), P("row", None)),
        check_vma=False,
    )
```

profile of v0, /device:TPU:0, one launch (start us, length us, event | category | flops | bytes accessed | tf_op | source)
XLA Modules:
  0.0 1102.3 jit_solution(3550992194655780149)
XLA Ops:
  7.2 2.3 slice_select_fusion
  15.0 35.0 %all-reduce.4.cloned.1.call-done = f32[2048,8]{1,0:T(8,128)} async-done(((f32[2048,8]{1,0:T(8,128)}), f32[2048,8]{1,0:T(8,128)}) %all-reduce.4.cloned.1.call-update) | async-done | bytes 65552 | tf_op jit(solution)/shard_map/psum | solution.py:12
  50.0 161.0 %all_gather.27 = f32[16384,8]{1,0:T(8,128)} all-gather(f32[2048,8]{1,0:T(8,128)} %all-reduce.4.cloned.1.call-done), channel_id=1, replica_groups=mesh['row'=8,'col'=4] {'row'}, dimensions={0}, use_global_device_ids=true | all-gather | bytes 589824 | tf_op jit(solution)/shard_map/all_gather | solution.py:27
  211.0 44.8 %slice_reduce_fusion = (f32[16384]{0:T(1024)S(1)}, f32[16384]{0:T(1024)S(1)}, f32[16384]{0:T(1024)S(1)}, f32[16384]{0:T(1024)S(1)}, f32[16384]{0:T(1024)S(1)}, /...) fusion(f32[16384,8]{1,0:T(8,128)} %all_gather.27), kind=kLoop, calls=%fused_computation.1 | loop fusion | bytes 1048576 | tf_op jit(solution)/shard_map/slice | solution.py:35
  259.0 1.9 fusion.5
  261.2 30.9 %fusion.109 = f32[1,2048]{1,0:T(1,128)S(1)} fusion(f32[4096,1]{0,1:T(1,128)S(1)} %bitcast.330, f32[2048,4096]{1,0:T(8,128)} %param.33), kind=kOutput, calls=%fused_computation.248 | convolution fusion | flops 100663296 | bytes 33579008 | tf_op jit(solution)/shard_map/dot_general | solution.py:16
  292.1 5.8 psum.120
  299.2 21.0 %psum.121 = f32[]{:T(128)} all-reduce(f32[]{:T(128)} %multiply_reduce_fusion.15), channel_id=1, replica_groups=mesh['row'=8,'col'=4] {'row'}, use_global_device_ids=true, to_apply=%region_7.8 | all-reduce | flops 1 | bytes 8 | tf_op jit(solution)/shard_map/psum | solution.py:55
  320.9 30.5 %all_gather.28 = f32[16384]{0:T(1024)S(1)} all-gather(f32[2048]{0:T(1024)S(1)} %multiply_subtract_fusion.7), channel_id=1, replica_groups=mesh['row'=8,'col'=4] {'row'}, dimensions={0}, use_global_device_ids=true | all-gather | bytes 73728 | tf_op jit(solution)/shard_map/all_gather | solution.py:57
  355.4 1.2 convolution_bitcast_fusion.12
  356.6 1.2 convolution_bitcast_fusion.13
  359.1 30.9 %fusion.110 = f32[1,2048]{1,0:T(1,128)S(1)} fusion(f32[4096,1]{0,1:T(1,128)S(1)} %bitcast.323, f32[2048,4096]{1,0:T(8,128)} %param.33), kind=kOutput, calls=%fused_computation.249 | convolution fusion | flops 100663296 | bytes 33579008 | tf_op jit(solution)/shard_map/dot_general | solution.py:16
  390.0 5.8 psum.122
  396.4 17.7 %psum.123 = f32[]{:T(128)} all-reduce(f32[]{:T(128)} %get-tuple-element.236), channel_id=1, replica_groups=mesh['row'=8,'col'=4] {'row'}, use_global_device_ids=true, to_apply=%region_13.14 | all-reduce | flops 1 | bytes 8 | tf_op jit(solution)/shard_map/psum | solution.py:55
  414.8 30.5 %all_gather.29 = f32[16384]{0:T(1024)S(1)} all-gather(f32[2048]{0:T(1024)S(1)} %multiply_subtract_fusion.6), channel_id=1, replica_groups=mesh['row'=8,'col'=4] {'row'}, dimensions={0}, use_global_device_ids=true | all-gather | bytes 73728 | tf_op jit(solution)/shard_map/all_gather | solution.py:57
  451.6 1.2 convolution_bitcast_fusion.11
  453.9 30.7 %fusion.111 = f32[1,2048]{1,0:T(1,128)S(1)} fusion(f32[4096,1]{0,1:T(1,128)S(1)} %bitcast.325, f32[2048,4096]{1,0:T(8,128)} %param.33), kind=kOutput, calls=%fused_computation.250 | convolution fusion | flops 100663296 | bytes 33579008 | tf_op jit(solution)/shard_map/dot_general | solution.py:16
  484.6 5.8 psum.124
  491.0 19.7 %psum.125 = f32[]{:T(128)} all-reduce(f32[]{:T(128)} %get-tuple-element.233), channel_id=1, replica_groups=mesh['row'=8,'col'=4] {'row'}, use_global_device_ids=true, to_apply=%region_19.20 | all-reduce | flops 1 | bytes 8 | tf_op jit(solution)/shard_map/psum | solution.py:55
  511.4 30.5 %all_gather.30 = f32[16384]{0:T(1024)S(1)} all-gather(f32[2048]{0:T(1024)S(1)} %multiply_subtract_fusion.5), channel_id=1, replica_groups=mesh['row'=8,'col'=4] {'row'}, dimensions={0}, use_global_device_ids=true | all-gather | bytes 73728 | tf_op jit(solution)/shard_map/all_gather | solution.py:57
  547.4 1.2 convolution_bitcast_fusion.8
  548.7 1.2 convolution_bitcast_fusion.9
  551.0 30.7 %fusion.112 = f32[1,2048]{1,0:T(1,128)S(1)} fusion(f32[4096,1]{0,1:T(1,128)S(1)} %bitcast.326, f32[2048,4096]{1,0:T(8,128)} %param.33), kind=kOutput, calls=%fused_computation.251 | convolution fusion | flops 100663296 | bytes 33579008 | tf_op jit(solution)/shard_map/dot_general | solution.py:16
  581.7 5.8 psum.126
  588.1 17.8 %psum.127 = f32[]{:T(128)} all-reduce(f32[]{:T(128)} %get-tuple-element.230), channel_id=1, replica_groups=mesh['row'=8,'col'=4] {'row'}, use_global_device_ids=true, to_apply=%region_25.26 | all-reduce | flops 1 | bytes 8 | tf_op jit(solution)/shard_map/psum | solution.py:55
  606.5 30.5 %all_gather.31 = f32[16384]{0:T(1024)S(1)} all-gather(f32[2048]{0:T(1024)S(1)} %multiply_subtract_fusion.4), channel_id=1, replica_groups=mesh['row'=8,'col'=4] {'row'}, dimensions={0}, use_global_device_ids=true | all-gather | bytes 73728 | tf_op jit(solution)/shard_map/all_gather | solution.py:57
  643.9 1.2 convolution_bitcast_fusion.7
  646.3 30.7 %fusion.113 = f32[1,2048]{1,0:T(1,128)S(1)} fusion(f32[4096,1]{0,1:T(1,128)S(1)} %bitcast.327, f32[2048,4096]{1,0:T(8,128)} %param.33), kind=kOutput, calls=%fused_computation.252 | convolution fusion | flops 100663296 | bytes 33579008 | tf_op jit(solution)/shard_map/dot_general | solution.py:16
  676.9 5.8 psum.128
  683.3 19.7 %psum.129 = f32[]{:T(128)} all-reduce(f32[]{:T(128)} %get-tuple-element.227), channel_id=1, replica_groups=mesh['row'=8,'col'=4] {'row'}, use_global_device_ids=true, to_apply=%region_31.32 | all-reduce | flops 1 | bytes 8 | tf_op jit(solution)/shard_map/psum | solution.py:55
  703.7 30.5 %all_gather.32 = f32[16384]{0:T(1024)S(1)} all-gather(f32[2048]{0:T(1024)S(1)} %multiply_subtract_fusion.3), channel_id=1, replica_groups=mesh['row'=8,'col'=4] {'row'}, dimensions={0}, use_global_device_ids=true | all-gather | bytes 73728 | tf_op jit(solution)/shard_map/all_gather | solution.py:57
  741.2 1.2 convolution_bitcast_fusion.5
  743.5 30.7 %fusion.114 = f32[1,2048]{1,0:T(1,128)S(1)} fusion(f32[4096,1]{0,1:T(1,128)S(1)} %bitcast.328, f32[2048,4096]{1,0:T(8,128)} %param.33), kind=kOutput, calls=%fused_computation.253 | convolution fusion | flops 100663296 | bytes 33579008 | tf_op jit(solution)/shard_map/dot_general | solution.py:16
  774.2 5.9 psum.130
  780.7 17.7 %psum.131 = f32[]{:T(128)} all-reduce(f32[]{:T(128)} %get-tuple-element.224), channel_id=1, replica_groups=mesh['row'=8,'col'=4] {'row'}, use_global_device_ids=true, to_apply=%region_37.38 | all-reduce | flops 1 | bytes 8 | tf_op jit(solution)/shard_map/psum | solution.py:55
  799.1 30.5 %all_gather.33 = f32[16384]{0:T(1024)S(1)} all-gather(f32[2048]{0:T(1024)S(1)} %multiply_subtract_fusion.2), channel_id=1, replica_groups=mesh['row'=8,'col'=4] {'row'}, dimensions={0}, use_global_device_ids=true | all-gather | bytes 73728 | tf_op jit(solution)/shard_map/all_gather | solution.py:57
  836.3 1.2 convolution_bitcast_fusion.3
  838.7 30.7 %fusion.115 = f32[1,2048]{1,0:T(1,128)S(1)} fusion(f32[4096,1]{0,1:T(1,128)S(1)} %bitcast.329, f32[2048,4096]{1,0:T(8,128)} %param.33), kind=kOutput, calls=%fused_computation.254 | convolution fusion | flops 100663296 | bytes 33579008 | tf_op jit(solution)/shard_map/dot_general | solution.py:16
  869.4 5.9 psum.132
  875.9 19.7 %psum.133 = f32[]{:T(128)} all-reduce(f32[]{:T(128)} %get-tuple-element.221), channel_id=1, replica_groups=mesh['row'=8,'col'=4] {'row'}, use_global_device_ids=true, to_apply=%region_42.43 | all-reduce | flops 1 | bytes 8 | tf_op jit(solution)/shard_map/psum | solution.py:55
  896.3 30.5 %all_gather.34 = f32[16384]{0:T(1024)S(1)} all-gather(f32[2048]{0:T(1024)S(1)} %multiply_subtract_fusion.1), channel_id=1, replica_groups=mesh['row'=8,'col'=4] {'row'}, dimensions={0}, use_global_device_ids=true | all-gather | bytes 73728 | tf_op jit(solution)/shard_map/all_gather | solution.py:57
  933.4 1.2 convolution_bitcast_fusion.1
  935.8 30.7 %fusion.116 = f32[1,2048]{1,0:T(1,128)S(1)} fusion(f32[4096,1]{0,1:T(1,128)S(1)} %bitcast.324, f32[2048,4096]{1,0:T(8,128)} %param.33), kind=kOutput, calls=%fused_computation.255 | convolution fusion | flops 100663296 | bytes 33579008 | tf_op jit(solution)/shard_map/dot_general | solution.py:16
  966.5 5.9 psum.134
  973.5 17.8 %psum.135 = f32[]{:T(128)} all-reduce(f32[]{:T(128)} %get-tuple-element.218), channel_id=1, replica_groups=mesh['row'=8,'col'=4] {'row'}, use_global_device_ids=true, to_apply=%region_47.48 | all-reduce | flops 1 | bytes 8 | tf_op jit(solution)/shard_map/psum | solution.py:55
  991.9 30.5 %all_gather.35 = f32[16384]{0:T(1024)S(1)} all-gather(f32[2048]{0:T(1024)S(1)} %multiply_subtract_fusion), channel_id=1, replica_groups=mesh['row'=8,'col'=4] {'row'}, dimensions={0}, use_global_device_ids=true | all-gather | bytes 73728 | tf_op jit(solution)/shard_map/all_gather | solution.py:57
  1023.2 30.3 %fusion.20 = f32[2048,4096]{1,0:T(8,128)} fusion(f32[2048,8]{0,1:T(8,128)S(1)} %constant_dynamic-slice_fusion, f32[16384,8]{0,1:T(8,128)S(1)} %scatter.79, s32[]{:T(128)S(6)} %select_n.125), kind=kOutput, calls=%fused_computation.51 | convolution fusion | flops 805306368 | bytes 33751044 | tf_op jit(solution)/shard_map/dot_general | solution.py:16
  1053.5 41.4 %subtract_subtract_fusion = f32[2048,4096]{1,0:T(8,128)} fusion(f32[2048,4096]{1,0:T(8,128)} %param.33, f32[2048,4096]{1,0:T(8,128)} %fusion.20, f32[16384,8]{0,1:T(8,128)S(1)} %scatter.76, s32[]{:T(128)S(6)} %select_n.125, f32[16384,8]{0,1:T(8,128)S(1)} %scatter.79, s32[]{:T(128)S(6)} %select_n.126), kind=kOutput, calls=%fused_computation | convolution fusion | flops 822083584 | bytes 100859912 | tf_op jit(solution)/shard_map/dot_general | solution.py:16
  (130 shorter events, 54.7 us)
Async XLA Ops:
  7.2 42.8 %all-reduce.4.cloned.1.call-start = ((), (), s32[]{:S(2)}) async-start(), calls=%async_computation | async-start | bytes 2097152 | tf_op jit(solution)/shard_map/psum | solution.py:12
  1023.2 71.7 %copy-start = (f32[2048,8]{0,1:T(8,128)}, f32[2048,8]{0,1:T(8,128)S(1)}, u32[]{:S(2)}) copy-start(f32[2048,8]{0,1:T(8,128)S(1)} %constant_dynamic-slice_fusion) | copy-start | bytes 196612
Sparse Core Ops, SparseCore 0:
  10.9 39.0 all-reduce.3
where the time goes:
time: 1110 us; the launch traced here: 1100 us
  blocking collectives  603 us (54%)
  matrix products  348 us (31%)
  local copies, waits for them, and re-layouts  57.5 us (5%)
  waiting for transfers between devices  35 us (3%)
  between operations  31.6 us (3%)
  other arithmetic  27.5 us (2%)
    dot_general x53, matrix products, precise_dot(): jnp.dot(operand, factor, precision=lax.Precision.HIGHEST, preferred_eleme...  348 us
    all_gather x8, blocking collectives, local(): update = lax.all_gather(update_rows, 'row', axis=0, tiled=True)  244 us
    all_gather x1, blocking collectives, local(): whole_panel = lax.all_gather(panel, 'row', axis=0, tiled=True)  161 us
    psum x8, blocking collectives, local(): inner_product = lax.psum(jnp.sum(pushed * vector_rows), 'row')  151 us
    psum x8, blocking collectives, local(): row_image = lax.psum(precise_dot(matrix, vector_cols), 'col')  46.5 us
    slice x1, local copies, waits for them, and re-layouts, local(): whole_panel[:, column] - precise_dot(reflect, companion[column])  44.8 us
    psum x1, waiting for transfers between devices, from_root(): return lax.psum(block, axis)  35 us
  transfers between devices with their start and end apart: 1, of which 1 were waited for; matrix products, arithmetic and copies ran while one was open for 0% of the time, Pallas kernels for 0%

commit v1 on v0

--- a/solution.py
+++ b/solution.py
@@ -24,7 +24,17 @@
     row_index = lax.axis_index("row")
     col_index = lax.axis_index("col")
     panel = from_root(matrix[:, :COLS], "col", 0)
-    whole_panel = lax.all_gather(panel, "row", axis=0, tiled=True)
+    num_devices = lax.axis_size("row")
+    leaves = [panel]
+    for dd in range(num_devices - 1):
+        leaves.append(
+            lax.ppermute(
+                leaves[-1], "row", [(q, (q + 1) % num_devices) for q in range(num_devices)]
+            )
+        )
+    whole_panel = jnp.roll(
+        jnp.concatenate(leaves[::-1], 0), (lax.axis_index("row") + 1) * panel.shape[0], axis=0
+    )
     all_ids = jnp.arange(whole_panel.shape[0], dtype=jnp.int32)
     reflect = jnp.zeros((N, COLS), jnp.float32)
     companion = jnp.zeros((N, COLS), jnp.float32)

time: 1110 us -> 952 us (0.86)
  blocking collectives: 603 us -> 444 us
  waiting for transfers between devices: 35 us -> 78.4 us
  local copies, waits for them, and re-layouts: 57.5 us -> 15.3 us
    all_gather x1 -> x0, blocking collectives: 161 us -> none  [local(): whole_panel = lax.all_gather(panel, 'row', axis=0, tiled=True)]
    slice x1, local copies, waits for them, and re-layouts: 44.8 us -> 1.01 us  [local(): whole_panel[:, column] - precise_dot(reflect, companion[column])]
    ppermute x0 -> x7, waiting for transfers between devices: none -> 42.8 us  [local(): lax.ppermute(leaves[-1], 'row', [(q, (q + 1) % num_devices) for q in rang...]
  transfers between devices with their start and end apart: 1 -> 8, of which waited for: 1 -> 8; matrix products, arithmetic and copies ran while one was open for 0% -> 1% of each run, Pallas kernels for 0% -> 0%
where the time goes in v1:
time: 952 us; the launch traced here: 944 us
  blocking collectives  444 us (47%)
  matrix products  347 us (36%)
  waiting for transfers between devices  78.4 us (8%)
  between operations  31.8 us (3%)
  other arithmetic  25.7 us (3%)
  local copies, waits for them, and re-layouts  15.3 us (2%)
    dot_general x53, matrix products, precise_dot(): jnp.dot(operand, factor, precision=lax.Precision.HIGHEST, preferred_eleme...  347 us
    all_gather x8, blocking collectives, local(): update = lax.all_gather(update_rows, 'row', axis=0, tiled=True)  246 us
    psum x8, blocking collectives, local(): inner_product = lax.psum(jnp.sum(pushed * vector_rows), 'row')  151 us
    psum x8, blocking collectives, local(): row_image = lax.psum(precise_dot(matrix, vector_cols), 'col')  46.9 us
    ppermute x7, waiting for transfers between devices, local(): lax.ppermute(leaves[-1], 'row', [(q, (q + 1) % num_devices) for q in rang...  42.8 us
    psum x1, waiting for transfers between devices, from_root(): return lax.psum(block, axis)  35.7 us
  transfers between devices with their start and end apart: 8, of which 8 were waited for; matrix products, arithmetic and copies ran while one was open for 1% of the time, Pallas kernels for 0%

profile of v1, /device:TPU:0, one launch (start us, length us, event | category | flops | bytes accessed | tf_op | source)
XLA Modules:
  0.0 944.1 jit_solution(16564251371993421541)
XLA Ops:
  7.2 1.3 slice.327
  9.5 35.7 %all-reduce.4.cloned.1.call-done = f32[2048,8]{0,1:T(8,128)} async-done(((f32[2048,8]{0,1:T(8,128)}), f32[2048,8]{0,1:T(8,128)}) %all-reduce.4.cloned.1.call-update) | async-done | bytes 65552 | tf_op jit(solution)/shard_map/psum | solution.py:12
  45.1 1.5 collective-permute-start
  46.6 5.7 collective-permute-done
  52.3 7.0 collective-permute-done.1
  59.3 7.0 collective-permute-done.2
  66.2 7.6 collective-permute-done.3
  73.8 7.0 collective-permute-done.4
  80.8 7.0 collective-permute-done.5
  93.1 1.6 collective-permute-done.6
  101.1 1.9 fusion.5
  103.2 30.7 %fusion.110 = f32[1,2048]{1,0:T(1,128)S(1)} fusion(f32[4096,1]{0,1:T(1,128)S(1)} %bitcast.347, f32[2048,4096]{1,0:T(8,128)} %param.33), kind=kOutput, calls=%fused_computation.258 | convolution fusion | flops 100663296 | bytes 33579008 | tf_op jit(solution)/shard_map/dot_general | solution.py:16
  133.9 5.9 psum.120
  141.1 20.8 %psum.121 = f32[]{:T(128)} all-reduce(f32[]{:T(128)} %multiply_reduce_fusion.15), channel_id=1, replica_groups=mesh['row'=8,'col'=4] {'row'}, use_global_device_ids=true, to_apply=%region_7.8 | all-reduce | flops 1 | bytes 8 | tf_op jit(solution)/shard_map/psum | solution.py:65
  162.6 30.7 %all_gather.24 = f32[16384]{0:T(1024)S(1)} all-gather(f32[2048]{0:T(1024)S(1)} %multiply_subtract_fusion.7), channel_id=1, replica_groups=mesh['row'=8,'col'=4] {'row'}, dimensions={0}, use_global_device_ids=true | all-gather | bytes 73728 | tf_op jit(solution)/shard_map/all_gather | solution.py:67
  198.5 1.2 convolution_bitcast_fusion.13
  200.9 30.7 %fusion.111 = f32[1,2048]{1,0:T(1,128)S(1)} fusion(f32[4096,1]{0,1:T(1,128)S(1)} %bitcast.340, f32[2048,4096]{1,0:T(8,128)} %param.33), kind=kOutput, calls=%fused_computation.259 | convolution fusion | flops 100663296 | bytes 33579008 | tf_op jit(solution)/shard_map/dot_general | solution.py:16
  231.6 5.9 psum.122
  238.1 17.7 %psum.123 = f32[]{:T(128)} all-reduce(f32[]{:T(128)} %get-tuple-element.228), channel_id=1, replica_groups=mesh['row'=8,'col'=4] {'row'}, use_global_device_ids=true, to_apply=%region_13.14 | all-reduce | flops 1 | bytes 8 | tf_op jit(solution)/shard_map/psum | solution.py:65
  256.5 30.9 %all_gather.25 = f32[16384]{0:T(1024)S(1)} all-gather(f32[2048]{0:T(1024)S(1)} %multiply_subtract_fusion.6), channel_id=1, replica_groups=mesh['row'=8,'col'=4] {'row'}, dimensions={0}, use_global_device_ids=true | all-gather | bytes 73728 | tf_op jit(solution)/shard_map/all_gather | solution.py:67
  293.1 1.2 convolution_bitcast_fusion.11
  295.5 30.7 %fusion.112 = f32[1,2048]{1,0:T(1,128)S(1)} fusion(f32[4096,1]{0,1:T(1,128)S(1)} %bitcast.342, f32[2048,4096]{1,0:T(8,128)} %param.33), kind=kOutput, calls=%fused_computation.260 | convolution fusion | flops 100663296 | bytes 33579008 | tf_op jit(solution)/shard_map/dot_general | solution.py:16
  326.2 5.9 psum.124
  332.7 19.7 %psum.125 = f32[]{:T(128)} all-reduce(f32[]{:T(128)} %get-tuple-element.225), channel_id=1, replica_groups=mesh['row'=8,'col'=4] {'row'}, use_global_device_ids=true, to_apply=%region_19.20 | all-reduce | flops 1 | bytes 8 | tf_op jit(solution)/shard_map/psum | solution.py:65
  353.1 30.7 %all_gather.26 = f32[16384]{0:T(1024)S(1)} all-gather(f32[2048]{0:T(1024)S(1)} %multiply_subtract_fusion.5), channel_id=1, replica_groups=mesh['row'=8,'col'=4] {'row'}, dimensions={0}, use_global_device_ids=true | all-gather | bytes 73728 | tf_op jit(solution)/shard_map/all_gather | solution.py:67
  390.3 1.2 convolution_bitcast_fusion.9
  392.7 30.7 %fusion.113 = f32[1,2048]{1,0:T(1,128)S(1)} fusion(f32[4096,1]{0,1:T(1,128)S(1)} %bitcast.343, f32[2048,4096]{1,0:T(8,128)} %param.33), kind=kOutput, calls=%fused_computation.261 | convolution fusion | flops 100663296 | bytes 33579008 | tf_op jit(solution)/shard_map/dot_general | solution.py:16
  423.3 5.9 psum.126
  429.8 17.8 %psum.127 = f32[]{:T(128)} all-reduce(f32[]{:T(128)} %get-tuple-element.222), channel_id=1, replica_groups=mesh['row'=8,'col'=4] {'row'}, use_global_device_ids=true, to_apply=%region_25.26 | all-reduce | flops 1 | bytes 8 | tf_op jit(solution)/shard_map/psum | solution.py:65
  448.3 30.7 %all_gather.27 = f32[16384]{0:T(1024)S(1)} all-gather(f32[2048]{0:T(1024)S(1)} %multiply_subtract_fusion.4), channel_id=1, replica_groups=mesh['row'=8,'col'=4] {'row'}, dimensions={0}, use_global_device_ids=true | all-gather | bytes 73728 | tf_op jit(solution)/shard_map/all_gather | solution.py:67
  487.7 30.7 %fusion.114 = f32[1,2048]{1,0:T(1,128)S(1)} fusion(f32[4096,1]{0,1:T(1,128)S(1)} %bitcast.344, f32[2048,4096]{1,0:T(8,128)} %param.33), kind=kOutput, calls=%fused_computation.262 | convolution fusion | flops 100663296 | bytes 33579008 | tf_op jit(solution)/shard_map/dot_general | solution.py:16
  518.4 5.9 psum.128
  524.9 19.7 %psum.129 = f32[]{:T(128)} all-reduce(f32[]{:T(128)} %get-tuple-element.219), channel_id=1, replica_groups=mesh['row'=8,'col'=4] {'row'}, use_global_device_ids=true, to_apply=%region_31.32 | all-reduce | flops 1 | bytes 8 | tf_op jit(solution)/shard_map/psum | solution.py:65
  545.3 30.9 %all_gather.28 = f32[16384]{0:T(1024)S(1)} all-gather(f32[2048]{0:T(1024)S(1)} %multiply_subtract_fusion.3), channel_id=1, replica_groups=mesh['row'=8,'col'=4] {'row'}, dimensions={0}, use_global_device_ids=true | all-gather | bytes 73728 | tf_op jit(solution)/shard_map/all_gather | solution.py:67
  585.3 30.7 %fusion.115 = f32[1,2048]{1,0:T(1,128)S(1)} fusion(f32[4096,1]{0,1:T(1,128)S(1)} %bitcast.345, f32[2048,4096]{1,0:T(8,128)} %param.33), kind=kOutput, calls=%fused_computation.263 | convolution fusion | flops 100663296 | bytes 33579008 | tf_op jit(solution)/shard_map/dot_general | solution.py:16
  616.0 5.9 psum.130
  622.4 17.8 %psum.131 = f32[]{:T(128)} all-reduce(f32[]{:T(128)} %get-tuple-element.216), channel_id=1, replica_groups=mesh['row'=8,'col'=4] {'row'}, use_global_device_ids=true, to_apply=%region_37.38 | all-reduce | flops 1 | bytes 8 | tf_op jit(solution)/shard_map/psum | solution.py:65
  640.9 30.7 %all_gather.29 = f32[16384]{0:T(1024)S(1)} all-gather(f32[2048]{0:T(1024)S(1)} %multiply_subtract_fusion.2), channel_id=1, replica_groups=mesh['row'=8,'col'=4] {'row'}, dimensions={0}, use_global_device_ids=true | all-gather | bytes 73728 | tf_op jit(solution)/shard_map/all_gather | solution.py:67
  680.3 30.7 %fusion.116 = f32[1,2048]{1,0:T(1,128)S(1)} fusion(f32[4096,1]{0,1:T(1,128)S(1)} %bitcast.346, f32[2048,4096]{1,0:T(8,128)} %param.33), kind=kOutput, calls=%fused_computation.264 | convolution fusion | flops 100663296 | bytes 33579008 | tf_op jit(solution)/shard_map/dot_general | solution.py:16
  711.0 5.9 psum.132
  717.5 19.7 %psum.133 = f32[]{:T(128)} all-reduce(f32[]{:T(128)} %get-tuple-element.213), channel_id=1, replica_groups=mesh['row'=8,'col'=4] {'row'}, use_global_device_ids=true, to_apply=%region_42.43 | all-reduce | flops 1 | bytes 8 | tf_op jit(solution)/shard_map/psum | solution.py:65
  737.9 30.7 %all_gather.30 = f32[16384]{0:T(1024)S(1)} all-gather(f32[2048]{0:T(1024)S(1)} %multiply_subtract_fusion.1), channel_id=1, replica_groups=mesh['row'=8,'col'=4] {'row'}, dimensions={0}, use_global_device_ids=true | all-gather | bytes 73728 | tf_op jit(solution)/shard_map/all_gather | solution.py:67
  777.6 30.7 %fusion.117 = f32[1,2048]{1,0:T(1,128)S(1)} fusion(f32[4096,1]{0,1:T(1,128)S(1)} %bitcast.341, f32[2048,4096]{1,0:T(8,128)} %param.33), kind=kOutput, calls=%fused_computation.265 | convolution fusion | flops 100663296 | bytes 33579008 | tf_op jit(solution)/shard_map/dot_general | solution.py:16
  808.3 5.9 psum.134
  815.3 17.8 %psum.135 = f32[]{:T(128)} all-reduce(f32[]{:T(128)} %get-tuple-element.210), channel_id=1, replica_groups=mesh['row'=8,'col'=4] {'row'}, use_global_device_ids=true, to_apply=%region_47.48 | all-reduce | flops 1 | bytes 8 | tf_op jit(solution)/shard_map/psum | solution.py:65
  833.7 30.8 %all_gather.31 = f32[16384]{0:T(1024)S(1)} all-gather(f32[2048]{0:T(1024)S(1)} %multiply_subtract_fusion), channel_id=1, replica_groups=mesh['row'=8,'col'=4] {'row'}, dimensions={0}, use_global_device_ids=true | all-gather | bytes 73728 | tf_op jit(solution)/shard_map/all_gather | solution.py:67
  865.0 30.3 %fusion.20 = f32[2048,4096]{1,0:T(8,128)} fusion(f32[2048,8]{0,1:T(8,128)S(1)} %constant_dynamic-slice_fusion.1, f32[16384,8]{0,1:T(8,128)S(1)} %scatter.79, s32[]{:T(128)S(6)} %select_n.140), kind=kOutput, calls=%fused_computation.42 | convolution fusion | flops 805306368 | bytes 33751044 | tf_op jit(solution)/shard_map/dot_general | solution.py:16
  895.4 41.4 %subtract_subtract_fusion = f32[2048,4096]{1,0:T(8,128)} fusion(f32[2048,4096]{1,0:T(8,128)} %param.33, f32[2048,4096]{1,0:T(8,128)} %fusion.20, f32[16384,8]{0,1:T(8,128)S(1)} %scatter.76, s32[]{:T(128)S(6)} %select_n.140, f32[16384,8]{0,1:T(8,128)S(1)} %scatter.79, s32[]{:T(128)S(6)} %select_n.141), kind=kOutput, calls=%fused_computation | convolution fusion | flops 822083584 | bytes 100859912 | tf_op jit(solution)/shard_map/dot_general | solution.py:16
  (161 shorter events, 63.9 us)
Async XLA Ops:
  7.2 38.0 %all-reduce.4.cloned.1.call-start = ((), (), s32[]{:S(2)}) async-start(), calls=%async_computation | async-start | bytes 131072 | tf_op jit(solution)/shard_map/psum | solution.py:12
  45.1 7.2 collective-permute-start
  52.3 7.0 collective-permute-start.1
  59.3 7.0 collective-permute-start.2
  66.2 7.6 collective-permute-start.3
  73.8 7.0 collective-permute-start.4
  80.8 7.0 collective-permute-start.5
  87.8 7.0 collective-permute-start.6
  865.0 71.7 %copy-start = (f32[2048,8]{0,1:T(8,128)}, f32[2048,8]{0,1:T(8,128)S(1)}, u32[]{:S(2)}) copy-start(f32[2048,8]{0,1:T(8,128)S(1)} %constant_dynamic-slice_fusion.1) | copy-start | bytes 196612
Sparse Core Ops, SparseCore 0:
  10.9 34.2 all-reduce.3
